TPU v7x, 512 devices: a whole 4x8x8 slice. The times are simulated.
512 devices in a mesh: ops: 8 (over x, core), sec: 64 (over z, y).
Axes of the slice: x: 4, y: 8, z: 8, core: 2. Of those that a mesh axis runs over, the one named last changes fastest.
Arguments:
- wavefunction: bfloat16 [256, 16, 128, 128], P('sec'), may hold values from -6 to 6
- left_ops: bfloat16 [32, 256, 128, 128], P('ops', 'sec'), may hold values from -0.5 to 0.5
- right_ops: bfloat16 [32, 256, 128, 128], P('ops', 'sec'), may hold values from -0.5 to 0.5
- site_weights: float32 [32, 16], P('ops'), may hold values from -1 to 1
- right_sector: int32 [256, 16], replicated, may hold values from 0 to 255, as said below
- left_dims: int32 [256], replicated, may hold values from 32 to 128
- right_dims: int32 [256], replicated, may hold values from 32 to 128
- basis: bfloat16 [4, 256, 16, 128, 128], P(None, 'sec', None, 'ops')
Outputs:
- sigma: bfloat16 [256, 16, 128, 128], P('sec', None, 'ops')
- correlations: float32 [4], replicated
Inputs may be any that keep to these rules, and one draw needn't show every extreme that they name: For each two-site state, right_sector maps the 256 left sectors one to one onto the 256 right sectors. Right sector r lies on index r // 4 of sec and left sector a on index a // 4; the slabs of one index of sec go to every index of sec, 1 slabs to each.
All inputs are finite; a program needn't handle non-finite values.
Results may differ from a plain program's by a relative error of at most 0.0055.
Values may be sent and summed in bfloat16 or wider, within the bound.
A program may use at most 128 MiB of HBM per device.

v0:
```python
import jax
import jax.numpy as jnp
from jax import lax
from jax.sharding import PartitionSpec as P


def lookup(values_table, positions):
    flattened = values_table.reshape(-1)
    matches = positions[..., None] == jnp.arange(flattened.shape[0], dtype=jnp.int32)
    return jnp.sum(jnp.where(matches, flattened, 0), axis=-1)


def per_device(
    wavefunction, left_ops, right_ops, site_weights, right_sector, left_dims, right_dims, basis
):
    sectors, state_count, block_width, _ = wavefunction.shape
    term_count = left_ops.shape[0]
    peers = lax.axis_size("sec")
    position = lax.axis_index("sec")
    sector_total = right_sector.shape[0]
    item_count = sectors * state_count
    capacity = item_count // peers
    slot_count = peers * capacity
    target_dev = (right_sector // sectors).reshape(peers, item_count)
    devices = jnp.arange(peers, dtype=jnp.int32)
    onehot = (target_dev[:, :, None] == devices[None, None, :]).astype(jnp.int32)
    earlier = jnp.cumsum(onehot, axis=1) - onehot
    rank_all = jnp.sum(earlier * onehot, axis=2)
    my_target = lax.dynamic_index_in_dim(target_dev, position, 0, keepdims=False)
    my_rank = lax.dynamic_index_in_dim(rank_all, position, 0, keepdims=False)
    my_slot = my_target * capacity + my_rank
    slot_match = my_slot[:, None] == jnp.arange(slot_count, dtype=jnp.int32)[None, :]
    source_item = jnp.sum(
        jnp.where(slot_match, jnp.arange(item_count, dtype=jnp.int32)[:, None], 0), axis=0
    )
    slot_used = jnp.any(slot_match, axis=0)
    indices = jnp.arange(block_width, dtype=jnp.int32)
    my_sectors = lax.dynamic_slice_in_dim(right_sector, position * sectors, sectors, 0)
    my_left_dims = lax.dynamic_slice_in_dim(left_dims, position * sectors, sectors, 0)
    paired_dims = lookup(right_dims, my_sectors)
    keep_mask = (indices[None, None, :, None] < my_left_dims[:, None, None, None]) & (
        indices[None, None, None, :] < paired_dims[:, :, None, None]
    )
    masked = jnp.where(keep_mask, wavefunction, jnp.zeros_like(wavefunction))
    owned = position * sectors + jnp.arange(sectors, dtype=jnp.int32)
    matches_right = right_sector[None, :, :] == owned[:, None, None]
    anchor = jnp.sum(
        jnp.where(matches_right, jnp.arange(sector_total, dtype=jnp.int32)[None, :, None], 0),
        axis=1,
    )
    anchor_dev = anchor // sectors
    anchor_item = anchor % sectors * state_count + jnp.arange(state_count, dtype=jnp.int32)[None, :]
    anchor_rank = lookup(rank_all, anchor_dev * item_count + anchor_item)
    gather_rows = (anchor_dev * capacity + anchor_rank).reshape(-1)
    anchor_dims = lookup(left_dims, anchor)
    own_dims = lax.dynamic_slice_in_dim(right_dims, position * sectors, sectors, 0)
    out_keep = (indices[None, None, :, None] < anchor_dims[:, :, None, None]) & (
        indices[None, None, None, :] < own_dims[:, None, None, None]
    )
    products = jnp.stack(
        [
            jnp.einsum(
                "jxy,jpyz->jpxz", left_ops[term], masked, preferred_element_type=jnp.float32
            ).astype(jnp.bfloat16)
            for term in range(term_count)
        ]
    )
    flattened = products.reshape(term_count, item_count, block_width, block_width)
    outgoing = jnp.take(flattened, source_item, axis=1) * slot_used[None, :, None, None].astype(
        jnp.bfloat16
    )
    incoming = lax.all_to_all(outgoing, "sec", split_axis=1, concat_axis=1, tiled=True)
    arrived = jnp.take(incoming, gather_rows, axis=1).reshape(
        term_count, sectors, state_count, block_width, block_width
    )
    partial_value = jnp.zeros((sectors, state_count, block_width, block_width), jnp.float32)
    for term in range(term_count):
        partial_value = (
            partial_value
            + jnp.einsum(
                "jpxy,jyz->jpxz", arrived[term], right_ops[term], preferred_element_type=jnp.float32
            )
            * site_weights[term][None, :, None, None]
        )
    partial_value = jnp.where(out_keep, partial_value, 0.0)
    sigma_block = lax.psum_scatter(partial_value, "ops", scatter_dimension=2, tiled=True).astype(
        jnp.bfloat16
    )
    local_correlation = jnp.einsum(
        "vjpxy,jpxy->v", basis, sigma_block, preferred_element_type=jnp.float32
    )
    correlations = lax.psum(local_correlation, ("ops", "sec"))
    return (sigma_block, correlations)


def solution(mesh):
    in_specs = (
        P("sec", None, None, None),
        P("ops", "sec", None, None),
        P("ops", "sec", None, None),
        P("ops", None),
        P(),
        P(),
        P(),
        P(None, "sec", None, "ops", None),
    )
    out_specs = (P("sec", None, "ops", None), P())
    return jax.shard_map(
        per_device, mesh=mesh, in_specs=in_specs, out_specs=out_specs, check_vma=False
    )
```

profile of v0, /device:TPU:1, one launch (start us, length us, event | category | flops | bytes accessed | tf_op | source)
XLA Modules:
  0.0 505.0 jit_solution(2333832717340481551)
XLA Ops:
  7.2 0.0 copy-start
  7.2 0.8 add_select_fusion.1
  8.0 0.1 copy.60
  8.1 0.1 reshape.157
  8.2 0.1 copy.61
  8.3 2.3 fusion.3
  10.5 0.2 add_reduce_fusion
  10.7 0.1 select_reduce_fusion.4
  10.8 0.1 fusion.26
  11.0 0.8 constant_dynamic-slice_fusion
  11.7 0.8 dynamic_slice.17
  12.5 0.1 iota_compare_fusion.8
  12.6 0.1 copy.64
  12.6 0.9 select_reduce_fusion.1
  13.5 0.1 iota_compare_fusion.6
  13.6 2.9 convolution_convert_fusion.2
  16.6 1.2 convolution_convert_fusion.1
  17.8 1.2 convolution_convert_fusion
  19.0 1.2 convolution_convert_fusion.3
  20.3 3.8 pad_maximum_fusion
  24.1 8.9 %gather_fusion = bf16[64,4,128,128]{2,3,1,0:T(8,128)(2,1)} fusion(bf16[4,64,128,128]{2,3,1,0:T(8,128)(2,1)} %pad_maximum_fusion, s32[1024]{0:T(1024)S(1)} %pad_clamp_fusion.1), kind=kCustom, calls=%fused_computation.clone | custom fusion | bytes 16777472 | tf_op jit(solution)/shard_map/jit(_take)/gather | solution.py:69
  33.0 7.5 %bitcast_multiply_fusion = bf16[4,64,128,128]{2,3,0,1:T(8,128)(2,1)} fusion(bf16[64,4,128,128]{2,3,1,0:T(8,128)(2,1)} %gather_fusion, pred[64]{0:T(512)(128)(4,1)S(1)} %compare_and_fusion.1, bf16[64]{0:T(256)(128)(2,1)S(1)} %convert_element_type.47), kind=kLoop, calls=%fused_computation.3 | loop fusion | flops 8388608 | bytes 16777408 | tf_op jit(solution)/shard_map/mul | solution.py:69
  40.5 17.5 %all-to-all-start = ((bf16[4,64,128,128]{2,3,0,1:T(8,128)(2,1)}), bf16[4,64,128,128]{2,3,0,1:T(8,128)(2,1)}, u32[]{:S(2)}, u32[]{:S(2)}) async-start(bf16[4,64,128,128]{2,3,0,1:T(8,128)(2,1)} %bitcast_multiply_fusion), calls=%async_computation | async-start | bytes 16777216 | tf_op jit(solution)/shard_map/all_to_all | solution.py:72
  58.0 0.2 reduce-scatter.2.cloned.1.call-start
  58.3 0.1 dynamic_slice.16
  58.4 0.1 copy.62
  58.4 0.2 select_reduce_fusion.3
  58.7 0.1 reduce_sum.63
  58.7 0.1 reshape.158
  58.8 0.3 select_reduce_fusion
  59.2 0.1 reduce_sum.65
  59.3 0.2 select_reduce_fusion.2
  59.5 0.1 iota_compare_fusion.9
  59.6 0.1 iota_compare_fusion.7
  59.7 254.2 %all-to-all-done = bf16[4,64,128,128]{2,3,0,1:T(8,128)(2,1)} async-done(((bf16[4,64,128,128]{2,3,0,1:T(8,128)(2,1)}), bf16[4,64,128,128]{2,3,0,1:T(8,128)(2,1)}, u32[]{:S(2)}, u32[]{:S(2)}) %all-to-all-start) | async-done | bytes 8388640 | tf_op jit(solution)/shard_map/all_to_all | solution.py:72
  313.9 8.9 %gather_fusion.1 = bf16[64,4,128,128]{2,3,1,0:T(8,128)(2,1)} fusion(bf16[4,64,128,128]{2,3,0,1:T(8,128)(2,1)} %all-to-all-done, s32[1024]{0:T(1024)S(1)} %pad_clamp_fusion), kind=kCustom, calls=%fused_computation.1.clone | custom fusion | bytes 16777472 | tf_op jit(solution)/shard_map/jit(_take)/gather | solution.py:73
  322.8 7.5 %select_bitcast_fusion = bf16[4,64,128,128]{2,3,0,1:T(8,128)(2,1)} fusion(bf16[64,4,128,128]{2,3,1,0:T(8,128)(2,1)} %gather_fusion.1, pred[64]{0:T(512)(128)(4,1)S(1)} %get-tuple-element.3), kind=kLoop, calls=%fused_computation.4 | loop fusion | flops 4194304 | bytes 16777280 | tf_op jit(solution)/shard_map/jit(_take)/select_n | solution.py:73
  330.3 3.9 fusion.39
  334.2 0.9 fusion.8
  335.1 0.9 fusion.10
  336.0 0.9 fusion.12
  336.9 5.0 add_select_fusion
  341.9 0.0 reduce-scatter.2.cloned.1.call-update
  341.9 52.5 %reduce-scatter.2.cloned.1.call-done = f32[4,16,16,128]{3,2,1,0:T(8,128)} async-done(((f32[4,16,128,128]{3,2,1,0:T(8,128)}), f32[4,16,16,128]{3,2,1,0:T(8,128)}) %reduce-scatter.2.cloned.1.call-update) | async-done | bytes 524304 | tf_op jit(solution)/shard_map/reduce_scatter | solution.py:86
  394.4 1.1 convert_bitcast_fusion
  395.5 1.6 convolution_bitcast_fusion
  397.1 100.3 %psum.7 = f32[4]{0:T(128)} all-reduce(f32[4]{0:T(128)S(1)} %convolution_bitcast_fusion), channel_id=1, replica_groups=mesh['ops'=8,'sec'=64] {'ops','sec'}, use_global_device_ids=true, to_apply=%region_9.11 | all-reduce | flops 4 | bytes 32 | tf_op jit(solution)/shard_map/psum | solution.py:92
  497.4 0.7 convert_element_type.48
  (26 shorter events, 0.1 us)
Async XLA Ops:
  7.2 388.3 %copy-start = (bf16[4,4,16,16,128]{4,3,2,1,0:T(8,128)(2,1)S(1)}, bf16[4,4,16,16,128]{4,3,2,1,0:T(8,128)(2,1)}, u32[]{:S(2)}) copy-start(bf16[4,4,16,16,128]{4,3,2,1,0:T(8,128)(2,1)} %param.17) | copy-start | bytes 3145732
  13.6 3.0 copy-start.7
  13.6 3.0 copy-start.8
  40.5 17.8 %copy-start.5 = (s32[256]{0:T(256)S(1)}, s32[256]{0:T(256)}, u32[]{:S(2)}) copy-start(s32[256]{0:T(256)} %param.16) | copy-start | bytes 3076
  40.5 18.0 %copy-start.3 = (s32[256,16]{0,1:T(8,128)S(1)}, s32[256,16]{0,1:T(8,128)}, u32[]{:S(2)}) copy-start(s32[256,16]{0,1:T(8,128)} %param.14) | copy-start | bytes 49156
  40.5 18.8 %copy-start.6 = (s32[256]{0:T(256)S(1)}, s32[256]{0:T(256)}, u32[]{:S(2)}) copy-start(s32[256]{0:T(256)} %param.15) | copy-start | bytes 3076
  40.5 19.1 %copy-start.4 = (f32[4,16]{1,0:T(4,128)S(1)}, f32[4,16]{1,0:T(4,128)}, u32[]{:S(2)}) copy-start(f32[4,16]{1,0:T(4,128)} %param.13) | copy-start | bytes 772
  40.5 273.4 %all-to-all-start = ((bf16[4,64,128,128]{2,3,0,1:T(8,128)(2,1)}), bf16[4,64,128,128]{2,3,0,1:T(8,128)(2,1)}, u32[]{:S(2)}, u32[]{:S(2)}) async-start(bf16[4,64,128,128]{2,3,0,1:T(8,128)(2,1)} %bitcast_multiply_fusion), calls=%async_computation | async-start | bytes 16777216 | tf_op jit(solution)/shard_map/all_to_all | solution.py:72
  58.0 336.4 %reduce-scatter.2.cloned.1.call-start = ((), (), s32[]{:S(2)}) async-start(), calls=%async_computation.2 | async-start | bytes 4718592 | tf_op jit(solution)/shard_map/reduce_scatter | solution.py:86
  330.3 4.0 copy-start.2
  395.5 102.0 %copy-start.1 = (f32[4,16,16,128]{3,2,1,0:T(8,128)S(1)}, f32[4,16,16,128]{3,2,1,0:T(8,128)}, u32[]{:S(2)}) copy-start(f32[4,16,16,128]{3,2,1,0:T(8,128)} %reduce-scatter.2.cloned.1.call-done) | copy-start | bytes 1572868
Sparse Core Ops, SparseCore 0:
  342.1 52.2 reduce-scatter.1
where the time goes:
time: 506 us; the launch traced here: 505 us
  waiting for transfers between devices  307 us (61%)
  blocking collectives  100 us (20%)
  other arithmetic  26 us (5%)
  local copies, waits for them, and re-layouts  24.1 us (5%)
  starting transfers between devices  17.8 us (4%)
  matrix products  15.9 us (3%)
  between operations  14.3 us (3%)
    all_to_all x1, waiting for transfers between devices, per_device(): lax.all_to_all(outgoing, 'sec', split_axis=1, concat_axis=1, tiled=True)  254 us
    psum x1, blocking collectives, per_device(): correlations = lax.psum(local_correlation, ('ops', 'sec'))  100 us
    reduce_scatter x1, waiting for transfers between devices, per_device(): lax.psum_scatter(partial_value, 'ops', scatter_dimension=2, tiled=True)  52.5 us
    all_to_all x1, starting transfers between devices, per_device(): lax.all_to_all(outgoing, 'sec', split_axis=1, concat_axis=1, tiled=True)  17.5 us
  transfers between devices with their start and end apart: 2, of which 2 were waited for; matrix products, arithmetic and copies ran while one was open for 0% of the time, Pallas kernels for 0%

commit v1 on v0

--- a/solution.py
+++ b/solution.py
@@ -89,7 +89,7 @@
     local_correlation = jnp.einsum(
         "vjpxy,jpxy->v", basis, sigma_block, preferred_element_type=jnp.float32
     )
-    correlations = lax.psum(local_correlation, ("ops", "sec"))
+    correlations = lax.psum(lax.psum(local_correlation, "sec"), "ops")
     return (sigma_block, correlations)
 
 

time: 506 us -> 565 us (1.12)
  blocking collectives: 100 us -> 159 us
    psum x1 -> x2, blocking collectives: 100 us -> 159 us  [per_device(): correlations = lax.psum(lax.psum(local_correlation, 'sec'), 'ops')]
where the time goes in v1:
time: 565 us; the launch traced here: 564 us
  waiting for transfers between devices  307 us (54%)
  blocking collectives  159 us (28%)
  other arithmetic  26 us (5%)
  local copies, waits for them, and re-layouts  24.1 us (4%)
  starting transfers between devices  17.8 us (3%)
  matrix products  15.9 us (3%)
  between operations  14.3 us (3%)
    all_to_all x1, waiting for transfers between devices, per_device(): lax.all_to_all(outgoing, 'sec', split_axis=1, concat_axis=1, tiled=True)  254 us
    psum x2, blocking collectives, per_device(): correlations = lax.psum(lax.psum(local_correlation, 'sec'), 'ops')  159 us
    reduce_scatter x1, waiting for transfers between devices, per_device(): lax.psum_scatter(partial_value, 'ops', scatter_dimension=2, tiled=True)  52.5 us
    all_to_all x1, starting transfers between devices, per_device(): lax.all_to_all(outgoing, 'sec', split_axis=1, concat_axis=1, tiled=True)  17.5 us
  transfers between devices with their start and end apart: 2, of which 2 were waited for; matrix products, arithmetic and copies ran while one was open for 0% of the time, Pallas kernels for 0%

profile of v1, /device:TPU:1, one launch (start us, length us, event | category | flops | bytes accessed | tf_op | source)
XLA Modules:
  0.0 564.2 jit_solution(340102954706253573)
XLA Ops:
  7.2 0.8 add_select_fusion.1
  8.0 0.1 copy.60
  8.1 0.1 reshape.157
  8.2 0.1 copy.61
  8.3 2.3 fusion.3
  10.5 0.2 add_reduce_fusion
  10.7 0.1 select_reduce_fusion.4
  10.8 0.1 fusion.26
  11.0 0.8 constant_dynamic-slice_fusion
  11.7 0.8 dynamic_slice.17
  12.5 0.1 iota_compare_fusion.8
  12.6 0.1 copy.64
  12.6 0.9 select_reduce_fusion.1
  13.5 0.1 iota_compare_fusion.6
  13.6 2.9 convolution_convert_fusion.2
  16.6 1.2 convolution_convert_fusion.1
  17.8 1.2 convolution_convert_fusion
  19.0 1.2 convolution_convert_fusion.3
  20.3 3.8 pad_maximum_fusion
  24.1 8.9 %gather_fusion = bf16[64,4,128,128]{2,3,1,0:T(8,128)(2,1)} fusion(bf16[4,64,128,128]{2,3,1,0:T(8,128)(2,1)} %pad_maximum_fusion, s32[1024]{0:T(1024)S(1)} %pad_clamp_fusion.1), kind=kCustom, calls=%fused_computation.clone | custom fusion | bytes 16777472 | tf_op jit(solution)/shard_map/jit(_take)/gather | solution.py:69
  33.0 7.5 %bitcast_multiply_fusion = bf16[4,64,128,128]{2,3,0,1:T(8,128)(2,1)} fusion(bf16[64,4,128,128]{2,3,1,0:T(8,128)(2,1)} %gather_fusion, pred[64]{0:T(512)(128)(4,1)S(1)} %compare_and_fusion.1, bf16[64]{0:T(256)(128)(2,1)S(1)} %convert_element_type.47), kind=kLoop, calls=%fused_computation.3 | loop fusion | flops 8388608 | bytes 16777408 | tf_op jit(solution)/shard_map/mul | solution.py:69
  40.5 17.5 %all-to-all-start = ((bf16[4,64,128,128]{2,3,0,1:T(8,128)(2,1)}), bf16[4,64,128,128]{2,3,0,1:T(8,128)(2,1)}, u32[]{:S(2)}, u32[]{:S(2)}) async-start(bf16[4,64,128,128]{2,3,0,1:T(8,128)(2,1)} %bitcast_multiply_fusion), calls=%async_computation | async-start | bytes 16777216 | tf_op jit(solution)/shard_map/all_to_all | solution.py:72
  58.0 0.2 reduce-scatter.2.cloned.1.call-start
  58.3 0.1 dynamic_slice.16
  58.4 0.1 copy.62
  58.4 0.2 select_reduce_fusion.3
  58.7 0.1 reduce_sum.63
  58.7 0.1 reshape.158
  58.8 0.3 select_reduce_fusion
  59.2 0.1 reduce_sum.65
  59.3 0.2 select_reduce_fusion.2
  59.5 0.1 iota_compare_fusion.9
  59.6 0.1 iota_compare_fusion.7
  59.7 254.2 %all-to-all-done = bf16[4,64,128,128]{2,3,0,1:T(8,128)(2,1)} async-done(((bf16[4,64,128,128]{2,3,0,1:T(8,128)(2,1)}), bf16[4,64,128,128]{2,3,0,1:T(8,128)(2,1)}, u32[]{:S(2)}, u32[]{:S(2)}) %all-to-all-start) | async-done | bytes 8388640 | tf_op jit(solution)/shard_map/all_to_all | solution.py:72
  313.9 8.9 %gather_fusion.1 = bf16[64,4,128,128]{2,3,1,0:T(8,128)(2,1)} fusion(bf16[4,64,128,128]{2,3,0,1:T(8,128)(2,1)} %all-to-all-done, s32[1024]{0:T(1024)S(1)} %pad_clamp_fusion), kind=kCustom, calls=%fused_computation.1.clone | custom fusion | bytes 16777472 | tf_op jit(solution)/shard_map/jit(_take)/gather | solution.py:73
  322.8 7.5 %select_bitcast_fusion = bf16[4,64,128,128]{2,3,0,1:T(8,128)(2,1)} fusion(bf16[64,4,128,128]{2,3,1,0:T(8,128)(2,1)} %gather_fusion.1, pred[64]{0:T(512)(128)(4,1)S(1)} %get-tuple-element.3), kind=kLoop, calls=%fused_computation.4 | loop fusion | flops 4194304 | bytes 16777280 | tf_op jit(solution)/shard_map/jit(_take)/select_n | solution.py:73
  330.3 3.9 fusion.39
  334.2 0.9 fusion.8
  335.1 0.9 fusion.10
  336.0 0.9 fusion.12
  336.9 5.0 add_select_fusion
  341.9 0.0 reduce-scatter.2.cloned.1.call-update
  341.9 52.5 %reduce-scatter.2.cloned.1.call-done = f32[4,16,16,128]{3,2,1,0:T(8,128)} async-done(((f32[4,16,128,128]{3,2,1,0:T(8,128)}), f32[4,16,16,128]{3,2,1,0:T(8,128)}) %reduce-scatter.2.cloned.1.call-update) | async-done | bytes 524304 | tf_op jit(solution)/shard_map/reduce_scatter | solution.py:86
  394.4 1.1 convert_bitcast_fusion
  395.5 1.6 convolution_bitcast_fusion
  397.1 116.0 %psum.14 = f32[4]{0:T(128)S(1)} all-reduce(f32[4]{0:T(128)S(1)} %convolution_bitcast_fusion), channel_id=1, replica_groups=mesh['ops'=8,'sec'=64] {'sec'}, use_global_device_ids=true, to_apply=%region_9.11 | all-reduce | flops 4 | bytes 32 | tf_op jit(solution)/shard_map/psum | solution.py:92
  513.2 43.4 %psum.15 = f32[4]{0:T(128)} all-reduce(f32[4]{0:T(128)S(1)} %psum.14), channel_id=1, replica_groups=mesh['ops'=8,'sec'=64] {'ops'}, use_global_device_ids=true, to_apply=%region_10.12 | all-reduce | flops 4 | bytes 32 | tf_op jit(solution)/shard_map/psum | solution.py:92
  556.6 0.7 convert_element_type.48
  (27 shorter events, 0.1 us)
Async XLA Ops:
  7.2 388.3 %copy-start = (bf16[4,4,16,16,128]{4,3,2,1,0:T(8,128)(2,1)S(1)}, bf16[4,4,16,16,128]{4,3,2,1,0:T(8,128)(2,1)}, u32[]{:S(2)}) copy-start(bf16[4,4,16,16,128]{4,3,2,1,0:T(8,128)(2,1)} %param.17) | copy-start | bytes 3145732
  13.6 3.0 copy-start.7
  13.6 3.0 copy-start.8
  40.5 17.8 %copy-start.5 = (s32[256]{0:T(256)S(1)}, s32[256]{0:T(256)}, u32[]{:S(2)}) copy-start(s32[256]{0:T(256)} %param.16) | copy-start | bytes 3076
  40.5 18.0 %copy-start.3 = (s32[256,16]{0,1:T(8,128)S(1)}, s32[256,16]{0,1:T(8,128)}, u32[]{:S(2)}) copy-start(s32[256,16]{0,1:T(8,128)} %param.14) | copy-start | bytes 49156
  40.5 18.8 %copy-start.6 = (s32[256]{0:T(256)S(1)}, s32[256]{0:T(256)}, u32[]{:S(2)}) copy-start(s32[256]{0:T(256)} %param.15) | copy-start | bytes 3076
  40.5 19.1 %copy-start.4 = (f32[4,16]{1,0:T(4,128)S(1)}, f32[4,16]{1,0:T(4,128)}, u32[]{:S(2)}) copy-start(f32[4,16]{1,0:T(4,128)} %param.13) | copy-start | bytes 772
  40.5 273.4 %all-to-all-start = ((bf16[4,64,128,128]{2,3,0,1:T(8,128)(2,1)}), bf16[4,64,128,128]{2,3,0,1:T(8,128)(2,1)}, u32[]{:S(2)}, u32[]{:S(2)}) async-start(bf16[4,64,128,128]{2,3,0,1:T(8,128)(2,1)} %bitcast_multiply_fusion), calls=%async_computation | async-start | bytes 16777216 | tf_op jit(solution)/shard_map/all_to_all | solution.py:72
  58.0 336.4 %reduce-scatter.2.cloned.1.call-start = ((), (), s32[]{:S(2)}) async-start(), calls=%async_computation.2 | async-start | bytes 4718592 | tf_op jit(solution)/shard_map/reduce_scatter | solution.py:86
  330.3 4.0 copy-start.2
  395.5 161.1 %copy-start.1 = (f32[4,16,16,128]{3,2,1,0:T(8,128)S(1)}, f32[4,16,16,128]{3,2,1,0:T(8,128)}, u32[]{:S(2)}) copy-start(f32[4,16,16,128]{3,2,1,0:T(8,128)} %reduce-scatter.2.cloned.1.call-done) | copy-start | bytes 1572868
Sparse Core Ops, SparseCore 0:
  342.1 52.2 reduce-scatter.1
